TPU v7x, 32 devices: a whole 2x2x4 slice. The times are simulated.
32 devices in a mesh: wide: 16 (over z, y, core), narrow: 2 (over x).
Axes of the slice: x: 2, y: 2, z: 4, core: 2. Of those that a mesh axis runs over, the one named last changes fastest.
Arguments:
- shocks: bfloat16 [64, 4096], replicated, may hold values from -6 to 6
- load_tiles: bfloat16 [32, 128, 128], P('narrow'), may hold values from -0.5 to 0.5
- load_index: int32 [32, 2], P('narrow'), may hold values from 0 to 31, as said below
- delta_tiles: bfloat16 [1024, 128, 128], P('wide'), may hold values from -0.09375 to 0.09375
- delta_index: int32 [256, 4], P('wide'), may hold values from 0 to 31, all different within a row
- base_value: float32 [32768], P('wide'), may hold values from -3 to 3
- trade_set: int32 [32768], P('wide'), may hold values from 0 to 2047, as said below
- set_slot: int32 [2048], replicated, may hold values from 0 to 2047, as said below
- default_step: int32 [64, 2048], P('narrow', 'wide'), may hold values from 0 to 7
Outputs:
- epe: float32 [2048], P('wide')
- default_loss: float32 [2048], P('wide')
Inputs may be any that keep to these rules, and one draw needn't show every extreme that they name: load_index[i] = (row block, column block); the column blocks of the tiles of narrow index j lie in j * 16 to (j + 1) * 16 - 1, and no pair repeats. `delta_index`: the 4 factor blocks of one trade block differ. `set_slot`: A permutation of the netting sets. `trade_set`: of the 2048 trades of one index of wide, at most 256 have sets of one owner (set_slot // 128); one owner gets exactly 256 from every index of wide.
All inputs are finite; a program needn't handle non-finite values.
Results may differ from a plain program's by a relative error of at most 0.00046.
Values may be sent and summed in bfloat16 or wider, within the bound.
A program may use at most 64 MiB of HBM per device.

v0:
```python
import jax
import jax.numpy as jnp
from jax import lax
from jax.sharding import PartitionSpec as P

BLOCK = 128
STEPS = 8
STEP = 3


def on_device(
    shocks,
    load_tiles,
    load_index,
    delta_tiles,
    delta_index,
    base_value,
    trade_set,
    set_slot,
    default_step,
):
    narrow_count = lax.axis_size("narrow")
    group = lax.axis_index("narrow")
    scen_total, width = shocks.shape
    blocks_all = width // BLOCK
    own_blocks = blocks_all // narrow_count
    shock_blocks = shocks.reshape(scen_total, blocks_all, BLOCK)
    picked = jnp.take(shock_blocks, load_index[:, 0], axis=1)
    loaded = jnp.einsum("sla,lab->slb", picked, load_tiles, preferred_element_type=jnp.float32)
    target = load_index[:, 1] - group * own_blocks
    placing = (target[:, None] == jnp.arange(own_blocks, dtype=jnp.int32)[None, :]).astype(
        jnp.float32
    )
    spread = jnp.einsum("slb,lc->scb", loaded, placing, precision=lax.Precision.HIGHEST)
    own_columns = lax.dynamic_slice_in_dim(shock_blocks, group * own_blocks, own_blocks, 1).astype(
        jnp.float32
    )
    moves_own = (own_columns + spread).astype(jnp.bfloat16).reshape(scen_total, own_blocks * BLOCK)
    moves = lax.all_to_all(moves_own, "narrow", split_axis=0, concat_axis=1, tiled=True)
    scen_dev = moves.shape[0]
    move_blocks = moves.reshape(scen_dev, blocks_all, BLOCK)
    tb_count, per_block = delta_index.shape
    gathered = jnp.take(move_blocks, delta_index.reshape(-1), axis=1).reshape(
        scen_dev, tb_count, per_block, BLOCK
    )
    tile_groups = delta_tiles.reshape(tb_count, per_block, BLOCK, BLOCK)
    valued = jnp.einsum("sbka,bkat->sbt", gathered, tile_groups, preferred_element_type=jnp.float32)
    values = valued.reshape(scen_dev, tb_count * BLOCK) + base_value[None, :]
    wide_count = lax.axis_size("wide")
    own_sets = default_step.shape[1]
    slots = jnp.take(set_slot, trade_set)
    owner = slots // own_sets
    local = slots % own_sets
    capacity = 2 * trade_set.shape[0] // wide_count
    owner_hits = (owner[:, None] == jnp.arange(wide_count, dtype=jnp.int32)[None, :]).astype(
        jnp.int32
    )
    position = jnp.sum(jnp.cumsum(owner_hits, axis=0) * owner_hits, axis=1) - 1
    target_slot = owner * capacity + position
    sent_values = (
        jnp.zeros((scen_dev, wide_count * capacity), jnp.float32).at[:, target_slot].set(values)
    )
    sent_ids = (
        jnp.full((1, wide_count * capacity), float(own_sets), jnp.float32)
        .at[0, target_slot]
        .set(local.astype(jnp.float32))
    )
    got_values, got_ids = (
        lax.all_to_all(sent_values, "wide", split_axis=1, concat_axis=1, tiled=True),
        lax.all_to_all(sent_ids, "wide", split_axis=1, concat_axis=1, tiled=True),
    )
    member = (got_ids[0][None, :] == jnp.arange(own_sets, dtype=jnp.float32)[:, None]).astype(
        jnp.float32
    )
    netted = jnp.einsum("sr,nr->sn", got_values, member, precision=lax.Precision.HIGHEST)
    exposure = jnp.maximum(netted, 0.0)
    default_hit = (default_step == STEP).astype(jnp.float32)
    totals = lax.psum(
        (jnp.sum(exposure, axis=0), jnp.sum(default_hit * exposure, axis=0)), "narrow"
    )
    scen_all = scen_dev * narrow_count
    return (totals[0] / scen_all, totals[1] * (STEPS / scen_all))


def solution(mesh):
    return jax.shard_map(
        on_device,
        mesh=mesh,
        in_specs=(
            P(),
            P("narrow", None, None),
            P("narrow", None),
            P("wide", None, None),
            P("wide", None),
            P("wide"),
            P("wide"),
            P(),
            P("narrow", "wide"),
        ),
        out_specs=(P("wide"), P("wide")),
        check_vma=False,
    )
```

profile of v0, /device:TPU:0, one launch (start us, length us, event | category | flops | bytes accessed | tf_op | source)
XLA Modules:
  0.0 80.2 jit_solution(11723574881305017320)
XLA Ops:
  0.6 1.3 %copy_bitcast_fusion = bf16[64,32,128]{2,0,1:T(8,128)(2,1)S(1)} fusion(bf16[64,4096]{1,0:T(8,128)(2,1)} %param.9), kind=kLoop, calls=%fused_computation.16 | loop fusion | bytes 1048576 | tf_op jit(solution)/shard_map/reshape | solution.py:27
  2.0 0.7 and_bitcast_fusion
  2.7 0.8 subtract_bitcast_fusion
  3.4 1.1 %copy.44 = bf16[8,8,32,128]{3,2,1,0:T(8,128)(2,1)S(1)} copy(bf16[8,8,32,128]{3,1,2,0:T(8,128)(2,1)} %bitcast.73) | data formatting | bytes 1048576
  4.6 0.6 gather_fusion.1
  5.2 1.4 %convolution_bitcast_fusion.1 = f32[64,16,128]{2,0,1:T(8,128)S(1)} fusion(bf16[16,128,128]{2,1,0:T(8,128)(2,1)} %param.10, bf16[16,64,128]{2,1,0:T(8,128)(2,1)S(1)} %gather_fusion.1, pred[16]{0:T(512)(128)(4,1)S(1)} %and_bitcast_fusion), kind=kOutput, calls=%fused_computation.9 | convolution fusion | flops 33685504 | bytes 1310736 | tf_op jit(solution)/shard_map/sla,lab->slb/dot_general | solution.py:29
  6.6 0.7 fusion.2
  7.3 0.8 %all_to_all.26 = bf16[2,32,2048]{2,1,0:T(8,128)(2,1)} reshape(bf16[64,16,128]{2,1,0:T(8,128)(2,1)S(1)} %fusion.2) | data formatting | bytes 524288 | tf_op jit(solution)/shard_map/all_to_all | solution.py:39
  8.1 4.2 %all-to-all-start = ((bf16[2,32,2048]{2,1,0:T(8,128)(2,1)}), bf16[2,32,2048]{2,1,0:T(8,128)(2,1)S(1)}, u32[]{:S(2)}, u32[]{:S(2)}) async-start(bf16[2,32,2048]{2,1,0:T(8,128)(2,1)} %all_to_all.26), calls=%async_computation | async-start | bytes 524288 | tf_op jit(solution)/shard_map/all_to_all | solution.py:39
  12.5 11.8 %gather_fusion = s32[2048]{0:T(1024)S(1)} fusion(s32[2048]{0:T(1024)S(1)} %copy-done.1, s32[2048]{0:T(1024)S(1)} %fusion.26), kind=kCustom, calls=%fused_computation | custom fusion | bytes 24576 | tf_op jit(solution)/shard_map/jit(_take)/gather | solution.py:51
  24.3 4.5 %reduce-window.6 = s32[16,16,128]{2,1,0:T(8,128)S(1)} reduce-window(s32[16,16,128]{2,1,0:T(8,128)S(1)} %fusion.18, s32[]{:T(128)} %constant.84.clone.1), window={size=1x1x128 pad=0_0x0_0x127_0}, to_apply=%region_0.1 | reduce-window | flops 4161536 | bytes 262148 | tf_op jit(solution)/shard_map/reduce-window
  28.8 0.4 slice_reduce_fusion
  29.3 0.2 reduce-window.9
  29.4 0.1 broadcast_add_fusion
  29.7 0.1 copy.29
  29.8 0.3 copy.32
  30.1 0.2 reshape.122
  30.3 0.1 copy.34
  30.4 0.7 gather_fusion.2
  31.1 0.5 convolution_bitcast_fusion.2
  31.6 0.3 copy.36
  31.9 7.0 %scatter_custom_fusion = f32[32,4096]{0,1:T(8,128)} fusion(s32[2048]{0:T(1024)S(1)} %compare_select_fusion, f32[2048,32]{1,0:T(8,128)S(1)} %copy.36, f32[]{:T(128)} %constant.64.clone.1), kind=kCustom, calls=%fused_computation.14 | custom fusion | bytes 524292 | tf_op jit(solution)/shard_map/scatter | solution.py:61
  39.0 3.0 %copy.37 = f32[32,16,256]{2,0,1:T(8,128)} copy(f32[32,16,256]{0,2,1:T(8,128)} %bitcast.71) | data formatting | bytes 1048576 | tf_op jit(solution)/shard_map/all_to_all | solution.py:69
  42.0 6.6 %all-to-all-start.1 = ((f32[32,16,256]{2,0,1:T(8,128)}), f32[32,16,256]{2,0,1:T(8,128)S(1)}, u32[]{:S(2)}, u32[]{:S(2)}) async-start(f32[32,16,256]{2,0,1:T(8,128)} %copy.37), calls=%async_computation.1 | async-start | bytes 1048576 | tf_op jit(solution)/shard_map/all_to_all | solution.py:69
  48.7 0.1 and_reduce_fusion
  48.9 8.6 %scatter_custom_fusion.1 = f32[4096]{0:T(1024)} fusion(s32[2048]{0:T(1024)S(1)} %broadcast_select_fusion, f32[2048]{0:T(1024)S(1)} %get-tuple-element.6, f32[]{:T(128)} %constant.99.clone.1), kind=kCustom, calls=%fused_computation.47 | custom fusion | bytes 16388
  57.5 5.4 %all-to-all-done.1 = f32[32,16,256]{2,0,1:T(8,128)S(1)} async-done(((f32[32,16,256]{2,0,1:T(8,128)}), f32[32,16,256]{2,0,1:T(8,128)S(1)}, u32[]{:S(2)}, u32[]{:S(2)}) %all-to-all-start.1) | async-done | bytes 524320 | tf_op jit(solution)/shard_map/all_to_all | solution.py:69
  62.9 4.2 %all-to-all-start.2 = ((f32[1,16,256]{2,0,1:T(1,128)}), f32[1,16,256]{2,0,1:T(1,128)S(1)}, u32[]{:S(2)}, u32[]{:S(2)}) async-start(f32[1,16,256]{2,0,1:T(1,128)} %bitcast.20), calls=%async_computation.2 | async-start | bytes 32768 | tf_op jit(solution)/shard_map/all_to_all | solution.py:70
  67.1 6.5 %all-to-all-done.2 = f32[1,16,256]{2,0,1:T(1,128)S(1)} async-done(((f32[1,16,256]{2,0,1:T(1,128)}), f32[1,16,256]{2,0,1:T(1,128)S(1)}, u32[]{:S(2)}, u32[]{:S(2)}) %all-to-all-start.2) | async-done | bytes 16416 | tf_op jit(solution)/shard_map/all_to_all | solution.py:70
  73.6 1.2 %select_reduce_fusion = (f32[128]{0:T(128)S(1)}, f32[128]{0:T(128)S(1)}) fusion(s32[32,128]{1,0:T(8,128)S(1)} %copy-done.7, f32[32,4096]{1,0:T(8,128)S(1)} %bitcast.77, f32[4096]{0:T(1024)S(1)} %bitcast.83), kind=kOutput, calls=%fused_computation.40 | convolution fusion | flops 201871104 | bytes 558080 | tf_op jit(solution)/shard_map/sr,nr->sn/dot_general | solution.py:75
  74.8 4.9 %all-reduce.1 = (f32[128]{0:T(128)S(1)}, f32[128]{0:T(128)S(1)}) all-reduce(f32[128]{0:T(128)S(1)} %get-tuple-element.3, f32[128]{0:T(128)S(1)} %get-tuple-element.2), channel_id=1, replica_groups=mesh['wide'=16,'narrow'=2] {'narrow'}, use_global_device_ids=true, to_apply=%region_6.7 | all-reduce | flops 256 | bytes 2048 | tf_op jit(solution)/shard_map/psum | solution.py:78
  79.7 0.5 broadcast_multiply_fusion
  (32 shorter events, 0.5 us)
Async XLA Ops:
  0.6 30.5 %copy-start = (bf16[64,128,128]{2,1,0:T(8,128)(2,1)S(1)}, bf16[64,128,128]{2,1,0:T(8,128)(2,1)}, u32[]{:S(2)}) copy-start(bf16[64,128,128]{2,1,0:T(8,128)(2,1)} %param.12) | copy-start | bytes 6291460
  4.6 7.8 %copy-start.4 = (s32[16,4]{0,1:T(4,128)S(1)}, s32[16,4]{0,1:T(4,128)}, u32[]{:S(2)}) copy-start(s32[16,4]{0,1:T(4,128)} %param.13) | copy-start | bytes 772
  4.6 7.8 %copy-start.2 = (s32[2048]{0:T(1024)S(1)}, s32[2048]{0:T(1024)}, u32[]{:S(2)}) copy-start(s32[2048]{0:T(1024)} %param.15) | copy-start | bytes 24580
  4.6 7.8 %copy-start.1 = (s32[2048]{0:T(1024)S(1)}, s32[2048]{0:T(1024)}, u32[]{:S(2)}) copy-start(s32[2048]{0:T(1024)} %param.16) | copy-start | bytes 24580
  8.1 21.7 %all-to-all-start = ((bf16[2,32,2048]{2,1,0:T(8,128)(2,1)}), bf16[2,32,2048]{2,1,0:T(8,128)(2,1)S(1)}, u32[]{:S(2)}, u32[]{:S(2)}) async-start(bf16[2,32,2048]{2,1,0:T(8,128)(2,1)} %all_to_all.26), calls=%async_computation | async-start | bytes 524288 | tf_op jit(solution)/shard_map/all_to_all | solution.py:39
  30.4 1.2 %copy-start.3 = (f32[2048]{0:T(1024)S(1)}, f32[2048]{0:T(1024)}, u32[]{:S(2)}) copy-start(f32[2048]{0:T(1024)} %param.14) | copy-start | bytes 24580
  39.0 9.7 %copy-start.5 = (s32[2]{0:T(128)S(1)}, s32[2]{0:T(128)}, u32[]{:S(2)}) copy-start(s32[2]{0:T(128)} %constant.106) | copy-start | bytes 28
  39.0 9.8 %copy-start.6 = (s32[2]{0:T(128)S(1)}, s32[2]{0:T(128)}, u32[]{:S(2)}) copy-start(s32[2]{0:T(128)} %constant.109) | copy-start | bytes 28
  39.0 34.6 %copy-start.7 = (s32[32,128]{1,0:T(8,128)S(1)}, s32[32,128]{1,0:T(8,128)}, u32[]{:S(2)}) copy-start(s32[32,128]{1,0:T(8,128)} %param.17) | copy-start | bytes 49156
  42.0 20.9 %all-to-all-start.1 = ((f32[32,16,256]{2,0,1:T(8,128)}), f32[32,16,256]{2,0,1:T(8,128)S(1)}, u32[]{:S(2)}, u32[]{:S(2)}) async-start(f32[32,16,256]{2,0,1:T(8,128)} %copy.37), calls=%async_computation.1 | async-start | bytes 1048576 | tf_op jit(solution)/shard_map/all_to_all | solution.py:69
  62.9 10.7 %all-to-all-start.2 = ((f32[1,16,256]{2,0,1:T(1,128)}), f32[1,16,256]{2,0,1:T(1,128)S(1)}, u32[]{:S(2)}, u32[]{:S(2)}) async-start(f32[1,16,256]{2,0,1:T(1,128)} %bitcast.20), calls=%async_computation.2 | async-start | bytes 32768 | tf_op jit(solution)/shard_map/all_to_all | solution.py:70
where the time goes:
time: 80.7 us; the launch traced here: 80.2 us
  local copies, waits for them, and re-layouts  36.6 us (45%)
  starting transfers between devices  15 us (19%)
  waiting for transfers between devices  11.9 us (15%)
  other arithmetic  7.14 us (9%)
  blocking collectives  4.93 us (6%)
  matrix products  3.71 us (5%)
  between operations  0.91 us (1%)
    gather x1, local copies, waits for them, and re-layouts, on_device(): slots = jnp.take(set_slot, trade_set)  11.8 us
    unnamed x19, local copies, waits for them, and re-layouts  9.88 us
    scatter x1, local copies, waits for them, and re-layouts, on_device(): jnp.zeros((scen_dev, wide_count * capacity), jnp.float32).at[:, target_slot]  7.03 us
    all_to_all x1, starting transfers between devices, on_device(): lax.all_to_all(sent_values, 'wide', split_axis=1, concat_axis=1, tiled=True)  6.63 us
    all_to_all x1, waiting for transfers between devices, on_device(): lax.all_to_all(sent_ids, 'wide', split_axis=1, concat_axis=1, tiled=True)  6.45 us
    all_to_all x1, waiting for transfers between devices, on_device(): lax.all_to_all(sent_values, 'wide', split_axis=1, concat_axis=1, tiled=True)  5.43 us
    psum x1, blocking collectives, on_device(): lax.psum((jnp.sum(exposure, axis=0), jnp.sum(default_hit * exposure, axis...  4.93 us
    another operation x3, other arithmetic  4.82 us
  transfers between devices with their start and end apart: 3, of which 2 were waited for; matrix products, arithmetic and copies ran while one was open for 33% of the time, Pallas kernels for 0%

commit v1 on v0

--- a/solution.py
+++ b/solution.py
@@ -6,6 +6,18 @@
 BLOCK = 128
 STEPS = 8
 STEP = 3
+
+
+def clear_quotas(shard_in):
+    return jnp.concatenate(
+        lax.all_to_all(
+            jnp.stack(jnp.split(shard_in, lax.axis_size("wide"), axis=1), axis=0),
+            axis_name="wide",
+            split_axis=0,
+            concat_axis=0,
+        ),
+        axis=1,
+    )
 
 
 def on_device(
@@ -66,7 +78,7 @@
         .set(local.astype(jnp.float32))
     )
     got_values, got_ids = (
-        lax.all_to_all(sent_values, "wide", split_axis=1, concat_axis=1, tiled=True),
+        clear_quotas(sent_values),
         lax.all_to_all(sent_ids, "wide", split_axis=1, concat_axis=1, tiled=True),
     )
     member = (got_ids[0][None, :] == jnp.arange(own_sets, dtype=jnp.float32)[:, None]).astype(

time: 80.7 us -> 102 us (1.26)
  local copies, waits for them, and re-layouts: 36.6 us -> 56.3 us
    another operation x0 -> x18, local copies, waits for them, and re-layouts: none -> 13 us  [clear_quotas(): jnp.stack(jnp.split(shard_in, lax.axis_size('wide'), axis=1), axis=0)]
    unnamed x19 -> x46, local copies, waits for them, and re-layouts: 9.88 us -> 19.7 us
    all_to_all x2 -> x0, local copies, waits for them, and re-layouts: 3.04 us -> none  [on_device(): lax.all_to_all(sent_values, 'wide', split_axis=1, concat_axis=1, tiled=True)]
  transfers between devices with their start and end apart: 3 -> 3, of which waited for: 2 -> 2; matrix products, arithmetic and copies ran while one was open for 33% -> 26% of each run, Pallas kernels for 0% -> 0%
where the time goes in v1:
time: 102 us; the launch traced here: 101 us
  local copies, waits for them, and re-layouts  56.3 us (55%)
  starting transfers between devices  15 us (15%)
  waiting for transfers between devices  11.9 us (12%)
  other arithmetic  7.79 us (8%)
  blocking collectives  4.93 us (5%)
  matrix products  4.42 us (4%)
    unnamed x46, local copies, waits for them, and re-layouts  19.7 us
    another operation x18, local copies, waits for them, and re-layouts, clear_quotas(): jnp.stack(jnp.split(shard_in, lax.axis_size('wide'), axis=1), axis=0)  13 us
    gather x1, local copies, waits for them, and re-layouts, on_device(): slots = jnp.take(set_slot, trade_set)  11.8 us
    scatter x1, local copies, waits for them, and re-layouts, on_device(): jnp.zeros((scen_dev, wide_count * capacity), jnp.float32).at[:, target_slot]  7.03 us
    all_to_all x1, starting transfers between devices, clear_quotas(): lax.all_to_all(jnp.stack(jnp.split(shard_in, lax.axis_size('wide'), axis=...  6.64 us
    all_to_all x1, waiting for transfers between devices, on_device(): lax.all_to_all(sent_ids, 'wide', split_axis=1, concat_axis=1, tiled=True)  6.45 us
    all_to_all x1, waiting for transfers between devices, clear_quotas(): lax.all_to_all(jnp.stack(jnp.split(shard_in, lax.axis_size('wide'), axis=...  5.43 us
    psum x1, blocking collectives, on_device(): lax.psum((jnp.sum(exposure, axis=0), jnp.sum(default_hit * exposure, axis...  4.93 us
  transfers between devices with their start and end apart: 3, of which 2 were waited for; matrix products, arithmetic and copies ran while one was open for 26% of the time, Pallas kernels for 0%

profile of v1, /device:TPU:0, one launch (start us, length us, event | category | flops | bytes accessed | tf_op | source)
XLA Modules:
  0.0 101.3 jit_solution(5487933590164059761)
XLA Ops:
  0.6 0.8 and_bitcast_fusion
  1.5 0.8 subtract_bitcast_fusion
  2.2 0.8 copy.48
  3.1 1.2 %copy_bitcast_fusion = bf16[64,32,128]{2,0,1:T(8,128)(2,1)S(1)} fusion(bf16[64,4096]{1,0:T(8,128)(2,1)} %param.9), kind=kLoop, calls=%fused_computation.16 | loop fusion | bytes 1048576 | tf_op jit(solution)/shard_map/reshape | solution.py:39
  4.3 1.1 %copy.74 = bf16[8,8,32,128]{3,2,1,0:T(8,128)(2,1)S(1)} copy(bf16[8,8,32,128]{3,1,2,0:T(8,128)(2,1)} %bitcast.106) | data formatting | bytes 1048576
  6.1 1.4 %convolution_bitcast_fusion.1 = f32[64,16,128]{2,0,1:T(8,128)S(1)} fusion(bf16[16,128,128]{2,1,0:T(8,128)(2,1)} %param.10, bf16[16,64,128]{2,1,0:T(8,128)(2,1)S(1)} %gather_fusion.1, pred[16]{0:T(512)(128)(4,1)S(1)} %and_bitcast_fusion), kind=kOutput, calls=%fused_computation.9 | convolution fusion | flops 33685504 | bytes 1310736 | tf_op jit(solution)/shard_map/sla,lab->slb/dot_general | solution.py:41
  7.5 0.7 fusion.2
  8.2 0.8 all_to_all.21
  9.0 4.2 %all-to-all-start = ((bf16[2,32,2048]{2,1,0:T(8,128)(2,1)}), bf16[2,32,2048]{2,1,0:T(8,128)(2,1)S(1)}, u32[]{:S(2)}, u32[]{:S(2)}) async-start(bf16[2,32,2048]{2,1,0:T(8,128)(2,1)} %all_to_all.21), calls=%async_computation | async-start | bytes 524288 | tf_op jit(solution)/shard_map/all_to_all | solution.py:51
  13.3 11.8 %gather_fusion = s32[2048]{0:T(1024)S(1)} fusion(s32[2048]{0:T(1024)S(1)} %copy-done.1, s32[2048]{0:T(1024)S(1)} %fusion.26), kind=kCustom, calls=%fused_computation | custom fusion | bytes 24576 | tf_op jit(solution)/shard_map/jit(_take)/gather | solution.py:63
  25.2 4.5 %reduce-window.6 = s32[16,16,128]{2,1,0:T(8,128)S(1)} reduce-window(s32[16,16,128]{2,1,0:T(8,128)S(1)} %fusion.18, s32[]{:T(128)} %constant.84.clone.1), window={size=1x1x128 pad=0_0x0_0x127_0}, to_apply=%region_0.1 | reduce-window | flops 4161536 | bytes 262148 | tf_op jit(solution)/shard_map/reduce-window
  31.1 0.7 gather_fusion.2
  32.6 7.0 %scatter_custom_fusion = f32[32,4096]{0,1:T(8,128)} fusion(s32[2048]{0:T(1024)S(1)} %compare_select_fusion, f32[2048,32]{1,0:T(8,128)S(1)} %copy.51, f32[]{:T(128)} %constant.64.clone.1), kind=kCustom, calls=%fused_computation.14 | custom fusion | bytes 524292 | tf_op jit(solution)/shard_map/scatter | solution.py:73
  39.6 2.5 %slice_bitcast_fusion = (f32[1,32,256]{1,2,0:T(8,128)}, f32[1,32,256]{1,2,0:T(8,128)}, f32[1,32,256]{1,2,0:T(8,128)}, f32[1,32,256]{1,2,0:T(8,128)}, f32[1,32,25...) fusion(f32[32,4096]{0,1:T(8,128)} %scatter_custom_fusion), kind=kLoop, calls=%fused_computation.29 | loop fusion | bytes 1048576 | tf_op jit(solution)/shard_map/stack | solution.py:14
  42.2 1.6 %copy.67 = f32[1,32,256]{2,1,0:T(8,128)} copy(f32[1,32,256]{1,2,0:T(8,128)} %get-tuple-element.6) | data formatting | bytes 65536 | tf_op jit(solution)/shard_map/stack | solution.py:14
  43.7 1.6 %copy.66 = f32[1,32,256]{2,1,0:T(8,128)} copy(f32[1,32,256]{1,2,0:T(8,128)} %get-tuple-element.7) | data formatting | bytes 65536 | tf_op jit(solution)/shard_map/stack | solution.py:14
  45.3 1.6 %copy.65 = f32[1,32,256]{2,1,0:T(8,128)} copy(f32[1,32,256]{1,2,0:T(8,128)} %get-tuple-element.8) | data formatting | bytes 65536 | tf_op jit(solution)/shard_map/stack | solution.py:14
  46.9 1.6 %copy.64 = f32[1,32,256]{2,1,0:T(8,128)} copy(f32[1,32,256]{1,2,0:T(8,128)} %get-tuple-element.9) | data formatting | bytes 65536 | tf_op jit(solution)/shard_map/stack | solution.py:14
  48.5 1.6 %copy.63 = f32[1,32,256]{2,1,0:T(8,128)} copy(f32[1,32,256]{1,2,0:T(8,128)} %get-tuple-element.10) | data formatting | bytes 65536 | tf_op jit(solution)/shard_map/stack | solution.py:14
  50.1 0.7 copy.62
  50.8 0.7 copy.61
  52.1 0.6 constant_dynamic-update-slice_fusion.15
  55.1 0.6 constant_dynamic-update-slice_fusion.10
  56.4 0.6 constant_dynamic-update-slice_fusion.8
  58.2 0.6 constant_dynamic-update-slice_fusion.5
  61.8 6.6 %all-to-all-start.1 = ((f32[16,32,256]{2,1,0:T(8,128)}), f32[16,32,256]{2,1,0:T(8,128)S(1)}, u32[]{:S(2)}, u32[]{:S(2)}) async-start(f32[16,32,256]{2,1,0:T(8,128)} %constant_dynamic-update-slice_fusion), calls=%async_computation.1 | async-start | bytes 1048576 | tf_op jit(solution)/shard_map/all_to_all | solution.py:13
  68.7 8.6 %scatter_custom_fusion.1 = f32[4096]{0:T(1024)} fusion(s32[2048]{0:T(1024)S(1)} %broadcast_select_fusion, f32[2048]{0:T(1024)S(1)} %get-tuple-element.22, f32[]{:T(128)} %constant.99.clone.1), kind=kCustom, calls=%fused_computation.79 | custom fusion | bytes 16388
  77.3 5.4 %all-to-all-done.1 = f32[16,32,256]{2,1,0:T(8,128)S(1)} async-done(((f32[16,32,256]{2,1,0:T(8,128)}), f32[16,32,256]{2,1,0:T(8,128)S(1)}, u32[]{:S(2)}, u32[]{:S(2)}) %all-to-all-start.1) | async-done | bytes 524320 | tf_op jit(solution)/shard_map/all_to_all | solution.py:13
  82.8 4.2 %all-to-all-start.2 = ((f32[1,16,256]{2,0,1:T(1,128)}), f32[1,16,256]{2,0,1:T(1,128)S(1)}, u32[]{:S(2)}, u32[]{:S(2)}) async-start(f32[1,16,256]{2,0,1:T(1,128)} %bitcast.36), calls=%async_computation.2 | async-start | bytes 32768 | tf_op jit(solution)/shard_map/all_to_all | solution.py:82
  87.0 6.5 %all-to-all-done.2 = f32[1,16,256]{2,0,1:T(1,128)S(1)} async-done(((f32[1,16,256]{2,0,1:T(1,128)}), f32[1,16,256]{2,0,1:T(1,128)S(1)}, u32[]{:S(2)}, u32[]{:S(2)}) %all-to-all-start.2) | async-done | bytes 16416 | tf_op jit(solution)/shard_map/all_to_all | solution.py:82
  93.4 1.9 %select_reduce_fusion = (f32[128]{0:T(128)S(1)}, f32[128]{0:T(128)S(1)}) fusion(s32[32,128]{1,0:T(8,128)} %param.17, f32[32,4096]{1,0:T(8,128)S(1)} %bitcast.110, f32[4096]{0:T(1024)S(1)} %bitcast.116), kind=kOutput, calls=%fused_computation.72 | convolution fusion | flops 201871104 | bytes 558080 | tf_op jit(solution)/shard_map/sr,nr->sn/dot_general | solution.py:87
  95.3 4.9 %all-reduce.1 = (f32[128]{0:T(128)S(1)}, f32[128]{0:T(128)S(1)}) all-reduce(f32[128]{0:T(128)S(1)} %get-tuple-element.3, f32[128]{0:T(128)S(1)} %get-tuple-element.2), channel_id=1, replica_groups=mesh['wide'=16,'narrow'=2] {'narrow'}, use_global_device_ids=true, to_apply=%region_6.7 | all-reduce | flops 256 | bytes 2048 | tf_op jit(solution)/shard_map/psum | solution.py:90
  (76 shorter events, 12.2 us)
Async XLA Ops:
  0.6 31.1 %copy-start = (bf16[64,128,128]{2,1,0:T(8,128)(2,1)S(1)}, bf16[64,128,128]{2,1,0:T(8,128)(2,1)}, u32[]{:S(2)}) copy-start(bf16[64,128,128]{2,1,0:T(8,128)(2,1)} %param.12) | copy-start | bytes 6291460
  5.4 7.8 %copy-start.11 = (s32[16,4]{0,1:T(4,128)S(1)}, s32[16,4]{0,1:T(4,128)}, u32[]{:S(2)}) copy-start(s32[16,4]{0,1:T(4,128)} %param.13) | copy-start | bytes 772
  5.4 7.9 %copy-start.9 = (s32[2048]{0:T(1024)S(1)}, s32[2048]{0:T(1024)}, u32[]{:S(2)}) copy-start(s32[2048]{0:T(1024)} %param.15) | copy-start | bytes 24580
  5.5 7.9 %copy-start.1 = (s32[2048]{0:T(1024)S(1)}, s32[2048]{0:T(1024)}, u32[]{:S(2)}) copy-start(s32[2048]{0:T(1024)} %param.16) | copy-start | bytes 24580
  9.0 21.5 %all-to-all-start = ((bf16[2,32,2048]{2,1,0:T(8,128)(2,1)}), bf16[2,32,2048]{2,1,0:T(8,128)(2,1)S(1)}, u32[]{:S(2)}, u32[]{:S(2)}) async-start(bf16[2,32,2048]{2,1,0:T(8,128)(2,1)} %all_to_all.21), calls=%async_computation | async-start | bytes 524288 | tf_op jit(solution)/shard_map/all_to_all | solution.py:51
  31.1 1.2 %copy-start.10 = (f32[2048]{0:T(1024)S(1)}, f32[2048]{0:T(1024)}, u32[]{:S(2)}) copy-start(f32[2048]{0:T(1024)} %param.14) | copy-start | bytes 24580
  50.7 8.7 %copy-start.5 = (f32[1,32,256]{2,1,0:T(8,128)S(1)}, f32[1,32,256]{2,1,0:T(8,128)}, u32[]{:S(2)}) copy-start(f32[1,32,256]{2,1,0:T(8,128)} %copy.64) | copy-start | bytes 98308
  50.7 9.3 %copy-start.4 = (f32[1,32,256]{2,1,0:T(8,128)S(1)}, f32[1,32,256]{2,1,0:T(8,128)}, u32[]{:S(2)}) copy-start(f32[1,32,256]{2,1,0:T(8,128)} %copy.65) | copy-start | bytes 98308
  50.7 9.9 %copy-start.3 = (f32[1,32,256]{2,1,0:T(8,128)S(1)}, f32[1,32,256]{2,1,0:T(8,128)}, u32[]{:S(2)}) copy-start(f32[1,32,256]{2,1,0:T(8,128)} %copy.66) | copy-start | bytes 98308
  50.7 10.5 %copy-start.2 = (f32[1,32,256]{2,1,0:T(8,128)S(1)}, f32[1,32,256]{2,1,0:T(8,128)}, u32[]{:S(2)}) copy-start(f32[1,32,256]{2,1,0:T(8,128)} %copy.67) | copy-start | bytes 98308
  51.4 6.1 %copy-start.8 = (f32[1,32,256]{2,1,0:T(8,128)S(1)}, f32[1,32,256]{2,1,0:T(8,128)}, u32[]{:S(2)}) copy-start(f32[1,32,256]{2,1,0:T(8,128)} %copy.61) | copy-start | bytes 98308
  51.4 6.8 %copy-start.7 = (f32[1,32,256]{2,1,0:T(8,128)S(1)}, f32[1,32,256]{2,1,0:T(8,128)}, u32[]{:S(2)}) copy-start(f32[1,32,256]{2,1,0:T(8,128)} %copy.62) | copy-start | bytes 98308
  51.4 7.4 %copy-start.6 = (f32[1,32,256]{2,1,0:T(8,128)S(1)}, f32[1,32,256]{2,1,0:T(8,128)}, u32[]{:S(2)}) copy-start(f32[1,32,256]{2,1,0:T(8,128)} %copy.63) | copy-start | bytes 98308
  51.6 16.9 %copy-start.12 = (s32[2]{0:T(128)S(1)}, s32[2]{0:T(128)}, u32[]{:S(2)}) copy-start(s32[2]{0:T(128)} %constant.106) | copy-start | bytes 28
  51.6 17.0 %copy-start.13 = (s32[2]{0:T(128)S(1)}, s32[2]{0:T(128)}, u32[]{:S(2)}) copy-start(s32[2]{0:T(128)} %constant.109) | copy-start | bytes 28
  61.8 20.9 %all-to-all-start.1 = ((f32[16,32,256]{2,1,0:T(8,128)}), f32[16,32,256]{2,1,0:T(8,128)S(1)}, u32[]{:S(2)}, u32[]{:S(2)}) async-start(f32[16,32,256]{2,1,0:T(8,128)} %constant_dynamic-update-slice_fusion), calls=%async_computation.1 | async-start | bytes 1048576 | tf_op jit(solution)/shard_map/all_to_all | solution.py:13
  82.8 10.7 %all-to-all-start.2 = ((f32[1,16,256]{2,0,1:T(1,128)}), f32[1,16,256]{2,0,1:T(1,128)S(1)}, u32[]{:S(2)}, u32[]{:S(2)}) async-start(f32[1,16,256]{2,0,1:T(1,128)} %bitcast.36), calls=%async_computation.2 | async-start | bytes 32768 | tf_op jit(solution)/shard_map/all_to_all | solution.py:82
